TPU v7x, 128 devices: a whole 4x4x4 slice. The times are simulated.
128 devices in a mesh: row: 8 (over z, core), col: 16 (over y, x).
Axes of the slice: x: 4, y: 4, z: 4, core: 2. Of those that a mesh axis runs over, the one named last changes fastest.
Arguments:
- snapshots: bfloat16 [4096, 32768], P('row', 'col'), may hold values from -14 to 14
- neighbours: int32 [4096, 128], P('row'), may hold values from 0 to 4095, all different within a row
- start_basis: float32 [32, 4096], replicated, may hold values from -6 to 6
Outputs:
- basis: float32 [32, 4096], P(None, 'row')
- rayleigh: float32 [32, 32], replicated
Inputs may be any that keep to these rules, and one draw needn't show every extreme that they name: `neighbours`: each row names 128 different snapshots.
All inputs are finite; a program needn't handle non-finite values.
Results may differ from a plain program's by a relative error of at most 0.00145.
Values may be sent and summed in bfloat16 or wider, within the bound.
No kernel may reach another device: no remote copies, remote signals or barrier semaphores. Data moves between devices by JAX's collectives and lax.ppermute only.
A program may use at most 128 MiB of HBM per device.

v0:
```python
import math
import jax
import jax.numpy as jnp
from jax import lax
from jax.sharding import PartitionSpec as P

FEATURES = 32768
LAGS = 64
ITERS = 2


def global_sum(value):
    return lax.psum(value, ("row", "col"))


def collect(columns):
    return lax.all_gather(columns, ("row", "col"), axis=1, tiled=True)


def shards(snapshots, neighbours, start_basis):
    row_count = lax.axis_size("row")
    col_count = lax.axis_size("col")
    row_at = lax.axis_index("row")
    col_at = lax.axis_index("col")
    lag_count = LAGS
    whole = lax.all_gather(snapshots, "row", axis=0, tiled=True)
    snap_count = whole.shape[0]
    feat_width = whole.shape[1]
    col_block = snap_count // col_count
    row_block = snapshots.shape[0]
    squares = jnp.sum(jnp.square(whole.astype(jnp.float32)), axis=1)
    padded_rows = jnp.concatenate([jnp.zeros((lag_count, feat_width), whole.dtype), whole], 0)
    padded_norms = jnp.concatenate([jnp.zeros((lag_count,), jnp.float32), squares], 0)
    row_start = row_at * row_block
    ext_rows = lax.dynamic_slice_in_dim(padded_rows, row_start, row_block + lag_count, 0)
    ext_norms = lax.dynamic_slice_in_dim(padded_norms, row_start, row_block + lag_count, 0)
    row_times = row_start - lag_count + jnp.arange(row_block + lag_count, dtype=jnp.int32)
    span = col_block + lag_count
    blocks = whole.reshape(col_count, col_block, feat_width)
    earlier = jnp.concatenate(
        [jnp.zeros((1, lag_count, feat_width), whole.dtype), blocks[:-1, col_block - lag_count :]],
        0,
    )
    source_rows = jnp.concatenate([earlier, blocks], 1).reshape(col_count * span, feat_width)
    norm_blocks = squares.reshape(col_count, col_block)
    norm_earlier = jnp.concatenate(
        [jnp.zeros((1, lag_count), jnp.float32), norm_blocks[:-1, col_block - lag_count :]], 0
    )
    source_norms = jnp.concatenate([norm_earlier, norm_blocks], 1).reshape(col_count * span)
    virtual = jnp.arange(span * lax.axis_size("col"), dtype=jnp.int32)
    times = virtual // span * col_block + virtual % span - lag_count
    inner = lax.dot_general(
        source_rows, ext_rows, (((1,), (1,)), ((), ())), preferred_element_type=jnp.float32
    )
    term = source_norms[:, None] + ext_norms[None, :] - 2.0 * inner
    keep = (times >= 0)[:, None] & (row_times >= 0)[None, :]
    tile = lax.psum_scatter(
        jnp.where(keep, term, 0.0).astype(jnp.bfloat16), "col", scatter_dimension=0, tiled=True
    ).astype(jnp.float32)
    window = 1
    while window < lag_count:
        tile = tile[window:, window:] + tile[:-window, :-window]
        window = window * 2
    lagged = tile[1:, 1:]
    step_rows = math.gcd(row_block, 16)
    block_count = row_block // step_rows
    slot_count = neighbours.shape[1]
    offset = neighbours - col_at * col_block
    inside = (offset >= 0) & (offset < col_block)
    tile_positions = jnp.arange(col_block, dtype=jnp.int32)

    def pick_block(pair):
        offs, lag_rows = pair
        match = offs[:, :, None] == tile_positions[None, None, :]
        return jnp.sum(jnp.where(match, lag_rows[:, None, :], 0.0), axis=2)

    chosen = lax.map(
        pick_block,
        (
            offset.reshape(block_count, step_rows, slot_count),
            lagged.T.reshape(block_count, step_rows, col_block),
        ),
    )
    chosen = chosen.reshape(row_block, slot_count)
    kernel_part = jnp.where(inside, 1.0 / (1.0 + chosen / (LAGS * FEATURES)), 0.0)
    slot_kernel = lax.psum(kernel_part, "col")
    mass = jnp.sum(slot_kernel, axis=1)
    markov = slot_kernel / mass[:, None]
    snap_positions = jnp.arange(snap_count, dtype=jnp.int32)

    def operator_block(pair):
        ids, weights = pair
        match = ids[:, :, None] == snap_positions[None, None, :]
        return jnp.sum(jnp.where(match, weights[:, :, None], 0.0), axis=1)

    transition = lax.map(
        operator_block,
        (
            neighbours.reshape(block_count, step_rows, slot_count),
            markov.reshape(block_count, step_rows, slot_count),
        ),
    )
    transition = transition.reshape(row_block, snap_count)
    piece_width = snap_count // (row_count * col_count)

    def apply_rows(basis_rows):
        return lax.dot_general(
            basis_rows,
            transition,
            (((1,), (1,)), ((), ())),
            precision=lax.Precision.HIGHEST,
            preferred_element_type=jnp.float32,
        )

    def own_piece(image):
        return lax.dynamic_slice_in_dim(image, col_at * piece_width, piece_width, 1)

    basis = start_basis
    for step in range(ITERS):
        piece = own_piece(apply_rows(basis))
        partial_gram = jnp.dot(
            piece, piece.T, precision=lax.Precision.HIGHEST, preferred_element_type=jnp.float32
        )
        gram_small = global_sum(partial_gram) / snap_count
        lower = jnp.linalg.cholesky(gram_small)
        basis = collect(jax.scipy.linalg.solve_triangular(lower, piece, lower=True))
    image_piece = own_piece(apply_rows(basis))
    basis_piece = lax.dynamic_slice_in_dim(
        basis, (row_at * col_count + col_at) * piece_width, piece_width, 1
    )
    partial_ray = jnp.dot(
        basis_piece,
        image_piece.T,
        precision=lax.Precision.HIGHEST,
        preferred_element_type=jnp.float32,
    )
    rayleigh = global_sum(partial_ray) / snap_count
    basis_rows = lax.dynamic_slice_in_dim(basis, row_start, row_block, 1)
    return (basis_rows, rayleigh)


def solution(mesh):
    placed = (P("row", "col"), P("row", None), P())
    return jax.shard_map(
        shards, mesh=mesh, in_specs=placed, out_specs=(P(None, "row"), P()), check_vma=False
    )
```

profile of v0, /device:TPU:1, one launch (start us, length us, event | category | flops | bytes accessed | tf_op | source)
XLA Modules:
  0.0 1007.9 jit_solution(16402256858035387622)
XLA Ops:
  8.0 90.6 %all-gather.2.cloned.1.call-done = bf16[4096,2048]{1,0:T(8,128)(2,1)} async-done(((bf16[512,2048]{1,0:T(8,128)(2,1)}), bf16[4096,2048]{1,0:T(8,128)(2,1)}) %all-gather.2.cloned.1.call-update) | async-done | bytes 16777232 | tf_op jit(solution)/shard_map/all_gather | solution.py:26
  108.7 21.4 %fusion.5 = bf16[16,320,2048]{2,1,0:T(8,128)(2,1)} fusion(bf16[15,64,2048]{2,1,0:T(8,128)(2,1)S(1)} %slice.69, bf16[16,256,2048]{2,1,0:T(8,128)(2,1)} %bitcast.64), kind=kLoop, calls=%fused_computation.15 | loop fusion | flops 62914560 | bytes 41680896 | tf_op jit(solution)/shard_map/concatenate | solution.py:44
  130.2 23.8 %select_convert_fusion = bf16[5120,576]{1,0:T(8,128)(2,1)} fusion(bf16[5120,2048]{1,0:T(8,128)(2,1)} %bitcast.70, f32[576]{0:T(1024)S(1)} %pad_dynamic-slice_fusion.2, f32[5120]{0:T(1024)S(1)} %add.130, pred[576]{0:T(1024)(128)(4,1)S(1)} %add_compare_fusion, pred[5120]{0:T(1024)(128)(4,1)S(1)} %fusion.17, s32[]{:T(128)S(6)} %select_n.56, ...), kind=kOutput, calls=%fused_computation.17 | convolution fusion | flops 12097290240 | bytes 43675460 | tf_op jit(solution)/shard_map/dot_general | solution.py:52
  154.1 80.7 %reduce-scatter.2.cloned.1.call-done = bf16[320,576]{1,0:T(8,128)(2,1)} async-done(((bf16[5120,576]{1,0:T(8,128)(2,1)}), bf16[320,576]{1,0:T(8,128)(2,1)}) %reduce-scatter.2.cloned.1.call-update) | async-done | bytes 368656 | tf_op jit(solution)/shard_map/reduce_scatter | solution.py:57
  238.1 28.1 %while.22 = (s32[]{:T(128)}, f32[32,16,128]{2,1,0:T(8,128)S(1)}, s32[32,16,128]{2,1,0:T(8,128)S(1)}, f32[32,16,256]{2,1,0:T(8,128)S(1)}, s32[]{:T(128)}) while((s32[]{:T(128)}, f32[32,16,128]{2,1,0:T(8,128)S(1)}, s32[32,16,128]{2,1,0:T(8,128)S(1)}, f32[32,16,256]{2,1,0:T(8,128)S(1)}, s32[]{:T(128)}) %tuple.63), condition=%wide.region_4.5_spmd.clone, body=%wide.region_2.4_spmd.clone.sunk | while | flops 1570818 | bytes 98377 | solution.py:77
  267.0 83.3 %all-reduce.6.cloned.1.call-done = f32[512,128]{1,0:T(8,128)} async-done(((f32[512,128]{1,0:T(8,128)}), f32[512,128]{1,0:T(8,128)}) %all-reduce.6.cloned.1.call-update) | async-done | bytes 262160 | tf_op jit(solution)/shard_map/psum | solution.py:86
  352.5 280.2 %while.23 = (s32[]{:T(128)}, f32[32,16,4096]{2,1,0:T(8,128)}, s32[32,16,128]{2,1,0:T(8,128)S(1)}, f32[32,16,128]{2,1,0:T(8,128)S(1)}, s32[]{:T(128)}) while((s32[]{:T(128)}, f32[32,16,4096]{2,1,0:T(8,128)}, s32[32,16,128]{2,1,0:T(8,128)S(1)}, f32[32,16,128]{2,1,0:T(8,128)S(1)}, s32[]{:T(128)}) %tuple.64), condition=%wide.region_9.10_spmd.clone, body=%wide.region_7.9_spmd.clone.sunk | while | flops 25100288 | bytes 836165 | solution.py:96
  361.3 8.0 select_reduce_fusion.6
  370.0 8.0 select_reduce_fusion.6
  378.8 8.0 select_reduce_fusion.6
  387.5 8.0 select_reduce_fusion.6
  396.3 8.0 select_reduce_fusion.6
  405.1 8.0 select_reduce_fusion.6
  413.8 8.0 select_reduce_fusion.6
  422.6 8.0 select_reduce_fusion.6
  431.4 8.0 select_reduce_fusion.6
  632.7 9.2 fusion.46
  642.1 65.8 %psum.29 = f32[32,32]{0,1:T(8,128)S(1)} all-reduce(f32[32,32]{0,1:T(8,128)S(1)} %fusion.36), channel_id=1, replica_groups=mesh['row'=8,'col'=16] {'row','col'}, use_global_device_ids=true, to_apply=%region_10.11 | all-reduce | flops 1024 | bytes 8192 | tf_op jit(solution)/shard_map/psum | solution.py:13
  714.8 63.7 %all_gather.10 = f32[32,4096]{0,1:T(8,128)S(1)} all-gather(f32[32,32]{0,1:T(8,128)S(1)} %fusion.23), channel_id=1, replica_groups=mesh['row'=8,'col'=16] {'row','col'}, dimensions={1}, use_global_device_ids=true | all-gather | bytes 528384 | tf_op jit(solution)/shard_map/all_gather | solution.py:17
  778.6 9.3 fusion.47
  788.1 65.0 %psum.30 = f32[32,32]{0,1:T(8,128)S(1)} all-reduce(f32[32,32]{0,1:T(8,128)S(1)} %fusion.33), channel_id=1, replica_groups=mesh['row'=8,'col'=16] {'row','col'}, use_global_device_ids=true, to_apply=%region_13.16 | all-reduce | flops 1024 | bytes 8192 | tf_op jit(solution)/shard_map/psum | solution.py:13
  860.2 65.1 %all_gather.11 = f32[32,4096]{0,1:T(8,128)S(1)} all-gather(f32[32,32]{0,1:T(8,128)S(1)} %fusion.20), channel_id=1, replica_groups=mesh['row'=8,'col'=16] {'row','col'}, dimensions={1}, use_global_device_ids=true | all-gather | bytes 528384 | tf_op jit(solution)/shard_map/all_gather | solution.py:17
  925.3 9.2 fusion.48
  934.8 65.0 %psum.31 = f32[32,32]{0,1:T(8,128)S(1)} all-reduce(f32[32,32]{0,1:T(8,128)S(1)} %fusion.29), channel_id=1, replica_groups=mesh['row'=8,'col'=16] {'row','col'}, use_global_device_ids=true, to_apply=%region_14.17 | all-reduce | flops 1024 | bytes 8192 | tf_op jit(solution)/shard_map/psum | solution.py:13
  (316 shorter events, 267.2 us)
Async XLA Ops:
  7.2 625.5 %copy-start = (f32[32,4096]{1,0:T(8,128)S(1)}, f32[32,4096]{1,0:T(8,128)}, u32[]{:S(2)}) copy-start(f32[32,4096]{1,0:T(8,128)} %param.12) | copy-start | bytes 1572868
  7.2 91.4 %all-gather.2.cloned.1.call-start = ((), (), s32[]{:S(2)}) async-start(), calls=%async_computation.1 | async-start | bytes 18874368 | tf_op jit(solution)/shard_map/all_gather | solution.py:26
  7.9 226.8 %reduce-scatter.2.cloned.1.call-start = ((), (), s32[]{:S(2)}) async-start(), calls=%async_computation.2 | async-start | bytes 6963200 | tf_op jit(solution)/shard_map/reduce_scatter | solution.py:57
  106.1 24.0 %slice-start = ((s8[16777216]{0:T(1024)(128)(4,1)}), s8[4194304]{0:T(1024)(128)(4,1)S(1)}, s32[]{:S(2)}) async-start(s8[16777216]{0:T(1024)(128)(4,1)} %bitcast.65), calls=%async_computation.4 | async-start | bytes 8388608
  108.7 21.5 %slice-start.1 = ((s8[16777216]{0:T(1024)(128)(4,1)}), s8[4194304]{0:T(1024)(128)(4,1)S(1)}, s32[]{:S(2)}) async-start(s8[16777216]{0:T(1024)(128)(4,1)} %bitcast.65), calls=%async_computation.5 | async-start | bytes 8388608
  108.7 21.4 %slice-start.2 = ((s8[16777216]{0:T(1024)(128)(4,1)}), s8[4194304]{0:T(1024)(128)(4,1)S(1)}, s32[]{:S(2)}) async-start(s8[16777216]{0:T(1024)(128)(4,1)} %bitcast.65), calls=%async_computation.6 | async-start | bytes 8388608
  108.7 21.4 %slice-start.3 = ((s8[16777216]{0:T(1024)(128)(4,1)}), s8[4194304]{0:T(1024)(128)(4,1)S(1)}, s32[]{:S(2)}) async-start(s8[16777216]{0:T(1024)(128)(4,1)} %bitcast.65), calls=%async_computation.7 | async-start | bytes 8388608
  130.1 23.9 %copy-start.1 = (s32[512,128]{1,0:T(8,128)S(1)}, s32[512,128]{1,0:T(8,128)}, u32[]{:S(2)}) copy-start(s32[512,128]{1,0:T(8,128)} %param.11) | copy-start | bytes 786436
  154.0 196.3 %all-reduce.6.cloned.1.call-start = ((), (), s32[]{:S(2)}) async-start(), calls=%async_computation.3 | async-start | bytes 524288 | tf_op jit(solution)/shard_map/psum | solution.py:86
Sparse Core Ops, SparseCore 0:
  9.7 88.8 all-gather.1
  154.1 80.6 reduce-scatter.1
  267.1 83.1 all-reduce.5
where the time goes:
time: 1020 us; the launch traced here: 1010 us
  other arithmetic  330 us (32%)
  blocking collectives  325 us (32%)
  waiting for transfers between devices  255 us (25%)
  matrix products  52.6 us (5%)
  local copies, waits for them, and re-layouts  29.2 us (3%)
  between operations  14.3 us (1%)
    reduce_sum x32, other arithmetic, operator_block(): return jnp.sum(jnp.where(match, weights[:, :, None], 0.0), axis=1)  256 us
    psum x3, blocking collectives, global_sum(): return lax.psum(value, ('row', 'col'))  196 us
    all_gather x2, blocking collectives, collect(): return lax.all_gather(columns, ('row', 'col'), axis=1, tiled=True)  129 us
    all_gather x1, waiting for transfers between devices, shards(): whole = lax.all_gather(snapshots, 'row', axis=0, tiled=True)  90.6 us
    psum x1, waiting for transfers between devices, shards(): slot_kernel = lax.psum(kernel_part, 'col')  83.3 us
    reduce_scatter x1, waiting for transfers between devices, shards(): lax.psum_scatter(jnp.where(keep, term, 0.0).astype(jnp.bfloat16), 'col',...  80.7 us
    dot_general x3, matrix products, apply_rows(): lax.dot_general(basis_rows, transition, (((1,), (1,)), ((), ())), precisi...  27.6 us
    reduce_sum x32, other arithmetic, pick_block(): return jnp.sum(jnp.where(match, lag_rows[:, None, :], 0.0), axis=2)  25.3 us
  transfers between devices with their start and end apart: 3, of which 3 were waited for; matrix products, arithmetic and copies ran while one was open for 0% of the time, Pallas kernels for 0%

commit v1 on v0

--- a/solution.py
+++ b/solution.py
@@ -83,7 +83,7 @@
     )
     chosen = chosen.reshape(row_block, slot_count)
     kernel_part = jnp.where(inside, 1.0 / (1.0 + chosen / (LAGS * FEATURES)), 0.0)
-    slot_kernel = lax.psum(kernel_part, "col")
+    slot_kernel = jnp.sum(lax.all_gather(kernel_part, "col"), 0)
     mass = jnp.sum(slot_kernel, axis=1)
     markov = slot_kernel / mass[:, None]
     snap_positions = jnp.arange(snap_count, dtype=jnp.int32)

time: 1020 us -> 986 us (0.967)
  waiting for transfers between devices: 255 us -> 224 us
    psum x1 -> x0, waiting for transfers between devices: 83.3 us -> none  [shards(): slot_kernel = lax.psum(kernel_part, 'col')]
    all_gather x0 -> x1, waiting for transfers between devices: none -> 52 us  [shards(): slot_kernel = jnp.sum(lax.all_gather(kernel_part, 'col'), 0)]
where the time goes in v1:
time: 986 us; the launch traced here: 979 us
  other arithmetic  333 us (34%)
  blocking collectives  324 us (33%)
  waiting for transfers between devices  224 us (23%)
  matrix products  52.3 us (5%)
  local copies, waits for them, and re-layouts  29.3 us (3%)
  between operations  14.3 us (1%)
    reduce_sum x32, other arithmetic, operator_block(): return jnp.sum(jnp.where(match, weights[:, :, None], 0.0), axis=1)  256 us
    psum x3, blocking collectives, global_sum(): return lax.psum(value, ('row', 'col'))  195 us
    all_gather x2, blocking collectives, collect(): return lax.all_gather(columns, ('row', 'col'), axis=1, tiled=True)  129 us
    all_gather x1, waiting for transfers between devices, shards(): whole = lax.all_gather(snapshots, 'row', axis=0, tiled=True)  90.6 us
    reduce_scatter x1, waiting for transfers between devices, shards(): lax.psum_scatter(jnp.where(keep, term, 0.0).astype(jnp.bfloat16), 'col',...  80.3 us
    all_gather x1, waiting for transfers between devices, shards(): slot_kernel = jnp.sum(lax.all_gather(kernel_part, 'col'), 0)  52 us
    dot_general x3, matrix products, apply_rows(): lax.dot_general(basis_rows, transition, (((1,), (1,)), ((), ())), precisi...  27.4 us
    reduce_sum x32, other arithmetic, pick_block(): return jnp.sum(jnp.where(match, lag_rows[:, None, :], 0.0), axis=2)  25.3 us
  transfers between devices with their start and end apart: 3, of which 3 were waited for; matrix products, arithmetic and copies ran while one was open for 0% of the time, Pallas kernels for 0%

profile of v1, /device:TPU:1, one launch (start us, length us, event | category | flops | bytes accessed | tf_op | source)
XLA Modules:
  0.0 979.2 jit_solution(11435574498841345638)
XLA Ops:
  8.0 90.6 %all-gather.4.cloned.1.call-done = bf16[4096,2048]{1,0:T(8,128)(2,1)} async-done(((bf16[512,2048]{1,0:T(8,128)(2,1)}), bf16[4096,2048]{1,0:T(8,128)(2,1)}) %all-gather.4.cloned.1.call-update) | async-done | bytes 16777232 | tf_op jit(solution)/shard_map/all_gather | solution.py:26
  108.7 21.4 %fusion.5 = bf16[16,320,2048]{2,1,0:T(8,128)(2,1)} fusion(bf16[15,64,2048]{2,1,0:T(8,128)(2,1)S(1)} %slice.69, bf16[16,256,2048]{2,1,0:T(8,128)(2,1)} %bitcast.65), kind=kLoop, calls=%fused_computation.15 | loop fusion | flops 62914560 | bytes 41680896 | tf_op jit(solution)/shard_map/concatenate | solution.py:44
  130.2 23.8 %select_convert_fusion = bf16[5120,576]{1,0:T(8,128)(2,1)} fusion(bf16[5120,2048]{1,0:T(8,128)(2,1)} %bitcast.71, f32[576]{0:T(1024)S(1)} %pad_dynamic-slice_fusion.2, f32[5120]{0:T(1024)S(1)} %add.128, pred[576]{0:T(1024)(128)(4,1)S(1)} %add_compare_fusion, pred[5120]{0:T(1024)(128)(4,1)S(1)} %fusion.17, s32[]{:T(128)S(6)} %select_n.56, ...), kind=kOutput, calls=%fused_computation.17 | convolution fusion | flops 12097290240 | bytes 43675460 | tf_op jit(solution)/shard_map/dot_general | solution.py:52
  154.5 80.3 %reduce-scatter.2.cloned.1.call-done = bf16[320,576]{1,0:T(8,128)(2,1)} async-done(((bf16[5120,576]{1,0:T(8,128)(2,1)}), bf16[320,576]{1,0:T(8,128)(2,1)}) %reduce-scatter.2.cloned.1.call-update) | async-done | bytes 368656 | tf_op jit(solution)/shard_map/reduce_scatter | solution.py:57
  238.2 27.6 %while.22 = (s32[]{:T(128)}, f32[32,16,128]{2,1,0:T(8,128)S(1)}, s32[32,16,128]{2,1,0:T(8,128)S(1)}, f32[32,16,256]{2,1,0:T(8,128)S(1)}, s32[]{:T(128)}) while((s32[]{:T(128)}, f32[32,16,128]{2,1,0:T(8,128)S(1)}, s32[32,16,128]{2,1,0:T(8,128)S(1)}, f32[32,16,256]{2,1,0:T(8,128)S(1)}, s32[]{:T(128)}) %tuple.63), condition=%wide.region_4.5_spmd.clone, body=%wide.region_2.4_spmd.clone.sunk | while | flops 1570818 | bytes 98377 | solution.py:77
  266.7 52.0 %all-gather.6.cloned.1.call-done = f32[8192,128]{1,0:T(8,128)} async-done(((f32[512,128]{1,0:T(8,128)}), f32[8192,128]{1,0:T(8,128)}) %all-gather.6.cloned.1.call-update) | async-done | bytes 4194320 | tf_op jit(solution)/shard_map/all_gather | solution.py:86
  324.7 280.2 %while.23 = (s32[]{:T(128)}, f32[32,16,4096]{2,1,0:T(8,128)}, s32[32,16,128]{2,1,0:T(8,128)S(1)}, f32[32,16,128]{2,1,0:T(8,128)S(1)}, s32[]{:T(128)}) while((s32[]{:T(128)}, f32[32,16,4096]{2,1,0:T(8,128)}, s32[32,16,128]{2,1,0:T(8,128)S(1)}, f32[32,16,128]{2,1,0:T(8,128)S(1)}, s32[]{:T(128)}) %tuple.61), condition=%wide.region_9.10_spmd.clone, body=%wide.region_7.9_spmd.clone.sunk | while | flops 25100288 | bytes 836165 | solution.py:96
  333.4 8.0 select_reduce_fusion.6
  342.2 8.0 select_reduce_fusion.6
  350.9 8.0 select_reduce_fusion.6
  359.7 8.0 select_reduce_fusion.6
  368.5 8.0 select_reduce_fusion.6
  377.2 8.0 select_reduce_fusion.6
  386.0 8.0 select_reduce_fusion.6
  394.7 8.0 select_reduce_fusion.6
  403.5 8.0 select_reduce_fusion.6
  604.9 9.1 fusion.46
  614.2 64.9 %psum.21 = f32[32,32]{0,1:T(8,128)S(1)} all-reduce(f32[32,32]{0,1:T(8,128)S(1)} %fusion.36), channel_id=1, replica_groups=mesh['row'=8,'col'=16] {'row','col'}, use_global_device_ids=true, to_apply=%region_10.11 | all-reduce | flops 1024 | bytes 8192 | tf_op jit(solution)/shard_map/psum | solution.py:13
  686.0 65.1 %all_gather.18 = f32[32,4096]{0,1:T(8,128)S(1)} all-gather(f32[32,32]{0,1:T(8,128)S(1)} %fusion.23), channel_id=1, replica_groups=mesh['row'=8,'col'=16] {'row','col'}, dimensions={1}, use_global_device_ids=true | all-gather | bytes 528384 | tf_op jit(solution)/shard_map/all_gather | solution.py:17
  751.2 9.3 fusion.47
  760.7 65.2 %psum.22 = f32[32,32]{0,1:T(8,128)S(1)} all-reduce(f32[32,32]{0,1:T(8,128)S(1)} %fusion.33), channel_id=1, replica_groups=mesh['row'=8,'col'=16] {'row','col'}, use_global_device_ids=true, to_apply=%region_13.16 | all-reduce | flops 1024 | bytes 8192 | tf_op jit(solution)/shard_map/psum | solution.py:13
  833.0 63.8 %all_gather.19 = f32[32,4096]{0,1:T(8,128)S(1)} all-gather(f32[32,32]{0,1:T(8,128)S(1)} %fusion.20), channel_id=1, replica_groups=mesh['row'=8,'col'=16] {'row','col'}, dimensions={1}, use_global_device_ids=true | all-gather | bytes 528384 | tf_op jit(solution)/shard_map/all_gather | solution.py:17
  896.8 9.0 fusion.48
  906.0 65.0 %psum.23 = f32[32,32]{0,1:T(8,128)S(1)} all-reduce(f32[32,32]{0,1:T(8,128)S(1)} %fusion.29), channel_id=1, replica_groups=mesh['row'=8,'col'=16] {'row','col'}, use_global_device_ids=true, to_apply=%region_14.17 | all-reduce | flops 1024 | bytes 8192 | tf_op jit(solution)/shard_map/psum | solution.py:13
  (320 shorter events, 271.5 us)
Async XLA Ops:
  7.2 597.7 %copy-start = (f32[32,4096]{1,0:T(8,128)S(1)}, f32[32,4096]{1,0:T(8,128)}, u32[]{:S(2)}) copy-start(f32[32,4096]{1,0:T(8,128)} %param.12) | copy-start | bytes 1572868
  7.2 91.4 %all-gather.4.cloned.1.call-start = ((), (), s32[]{:S(2)}) async-start(), calls=%async_computation.1 | async-start | bytes 18874368 | tf_op jit(solution)/shard_map/all_gather | solution.py:26
  7.9 226.9 %reduce-scatter.2.cloned.1.call-start = ((), (), s32[]{:S(2)}) async-start(), calls=%async_computation.2 | async-start | bytes 6963200 | tf_op jit(solution)/shard_map/reduce_scatter | solution.py:57
  106.1 24.0 %slice-start = ((s8[16777216]{0:T(1024)(128)(4,1)}), s8[4194304]{0:T(1024)(128)(4,1)S(1)}, s32[]{:S(2)}) async-start(s8[16777216]{0:T(1024)(128)(4,1)} %bitcast.66), calls=%async_computation.4 | async-start | bytes 8388608
  108.7 21.5 %slice-start.1 = ((s8[16777216]{0:T(1024)(128)(4,1)}), s8[4194304]{0:T(1024)(128)(4,1)S(1)}, s32[]{:S(2)}) async-start(s8[16777216]{0:T(1024)(128)(4,1)} %bitcast.66), calls=%async_computation.5 | async-start | bytes 8388608
  108.7 21.4 %slice-start.2 = ((s8[16777216]{0:T(1024)(128)(4,1)}), s8[4194304]{0:T(1024)(128)(4,1)S(1)}, s32[]{:S(2)}) async-start(s8[16777216]{0:T(1024)(128)(4,1)} %bitcast.66), calls=%async_computation.6 | async-start | bytes 8388608
  108.7 21.4 %slice-start.3 = ((s8[16777216]{0:T(1024)(128)(4,1)}), s8[4194304]{0:T(1024)(128)(4,1)S(1)}, s32[]{:S(2)}) async-start(s8[16777216]{0:T(1024)(128)(4,1)} %bitcast.66), calls=%async_computation.7 | async-start | bytes 8388608
  130.1 24.3 %copy-start.1 = (s32[512,128]{1,0:T(8,128)S(1)}, s32[512,128]{1,0:T(8,128)}, u32[]{:S(2)}) copy-start(s32[512,128]{1,0:T(8,128)} %param.11) | copy-start | bytes 786436
  154.0 164.7 %all-gather.6.cloned.1.call-start = ((), (), s32[]{:S(2)}) async-start(), calls=%async_computation.3 | async-start | bytes 4456448 | tf_op jit(solution)/shard_map/all_gather | solution.py:86
Sparse Core Ops, SparseCore 0:
  9.7 88.8 all-gather.3
  154.1 80.7 reduce-scatter.1
  266.8 51.8 all-gather.5
